TPU v7x, 32 devices: a whole 2x2x4 slice. The times are simulated.
32 devices in a mesh: seabed: 8 (over y, x, core), freq: 4 (over z).
Axes of the slice: x: 2, y: 2, z: 4, core: 2. Of those that a mesh axis runs over, the one named last changes fastest.
Arguments:
- uplift: bfloat16 [128, 32, 40, 128], P('freq', None, 'seabed'), may hold values from -6 to 6
- coefficient: float32 [40, 128], P('seabed'), may hold values from 0.06 to 0.24
- transfer: float32 [4, 2, 600, 5120], P('freq', None, None, 'seabed'), may hold values from -0.0625 to 0.0625
Outputs:
- sensors: float32 [128, 4, 2, 600], P('seabed', 'freq')
All inputs are finite; a program needn't handle non-finite values.
Results may differ from a plain program's by a relative error of at most 0.0003.
Values sent between devices are 32-bit elements; how exact they have to be, the bound alone decides.
No kernel may reach another device: no remote copies, remote signals or barrier semaphores. Data moves between devices by JAX's collectives and lax.ppermute only.
A program may use at most 64 MiB of HBM per device.

v0:
```python
import math
import jax
import jax.numpy as jnp
from jax import lax
from jax.sharding import PartitionSpec as P

FD = 1
PASSES = 3


def with_halo(block, sides, width):
    for axis, dim in sides:
        count = lax.axis_size(axis)
        forward = [(i, i + 1) for i in range(count - 1)]
        backward = [(target, source) for source, target in forward]
        low = lax.ppermute(
            lax.slice_in_dim(block, block.shape[dim] - width, None, axis=dim), axis, forward
        )
        high = lax.ppermute(lax.slice_in_dim(block, 0, width, axis=dim), axis, backward)
        block = jnp.concatenate([low, block, high], axis=dim)
    return block


def dft_table(steps_count, freq_count):
    times = jnp.arange(steps_count, dtype=jnp.int32)
    freqs = jnp.arange(freq_count, dtype=jnp.int32)
    phase = (freqs[:, None] * times[None, :] % steps_count).astype(jnp.float32) * (
        2.0 * math.pi / steps_count
    )
    scale = 1.0 / math.sqrt(steps_count)
    return (
        jnp.stack([jnp.cos(phase), -jnp.sin(phase)], 1).reshape(2 * freq_count, steps_count) * scale
    )


def relax(extended, rows_coefficient):
    centre = extended[:, :, 1:-1]
    padded = jnp.pad(centre, ((0, 0), (0, 0), (0, 0), (1, 1)))
    beside = extended[:, :, 2:] + extended[:, :, :-2] + padded[:, :, :, 2:] + padded[:, :, :, :-2]
    return centre + rows_coefficient * (beside - 4.0 * centre)


def shards(uplift, coefficient, transfer):
    field = uplift.astype(jnp.float32)
    vectors, steps_count, rows, width = field.shape
    extended = with_halo(field, (("seabed", 2),), PASSES)
    coefficient_rim = with_halo(coefficient, (("seabed", 0),), PASSES - 1)
    for step in range(PASSES):
        span = rows + 2 * (PASSES - 1 - step)
        extended = relax(extended, coefficient_rim[step : step + span])
    field = extended
    flat = field.reshape(vectors, steps_count, rows * width)
    freq_count = FD * lax.axis_size("freq")
    table = dft_table(steps_count, freq_count)
    spectrum = jnp.einsum("ft,vtc->fvc", table, flat, precision=lax.Precision.HIGHEST)
    spectrum = spectrum.reshape(freq_count, 2, vectors, rows * width)
    regrouped = lax.all_to_all(spectrum, "freq", split_axis=0, concat_axis=2, tiled=True)
    products = jnp.einsum("kbvc,kasc->vkbas", regrouped, transfer, precision=lax.Precision.HIGHEST)
    real_part = products[:, :, 0, 0] - products[:, :, 1, 1]
    imag_part = products[:, :, 1, 0] + products[:, :, 0, 1]
    return lax.psum_scatter(
        jnp.stack([real_part, imag_part], 2), "seabed", scatter_dimension=0, tiled=True
    )


def solution(mesh):
    placed = (P("freq", None, "seabed", None), P("seabed", None), P("freq", None, None, "seabed"))
    return jax.shard_map(
        shards,
        mesh=mesh,
        in_specs=placed,
        out_specs=P("seabed", "freq", None, None),
        check_vma=False,
    )
```

profile of v0, /device:TPU:0, one launch (start us, length us, event | category | flops | bytes accessed | tf_op | source)
XLA Modules:
  0.0 159.0 jit_solution(17470392824723948402)
XLA Ops:
  6.5 2.0 %fusion.34 = (f32[32,32,3,128]{3,1,2,0:T(8,128)S(1)}, f32[32,32,3,128]{3,1,2,0:T(8,128)S(1)}) fusion(bf16[32,32,5,128]{3,1,2,0:T(8,128)(2,1)} %param.3), kind=kLoop, calls=%fused_computation.51 | loop fusion | bytes 6291456 | tf_op jit(solution)/shard_map/slice | solution.py:17
  8.5 2.5 %collective-permute-start = (f32[32,32,3,128]{3,1,2,0:T(8,128)S(1)}, f32[32,32,3,128]{3,1,2,0:T(8,128)S(1)}, u32[]{:S(2)}, u32[]{:S(2)}) collective-permute-start(f32[32,32,3,128]{3,1,2,0:T(8,128)S(1)} %get-tuple-element.5), channel_id=1, source_target_pairs={{0,4},{4,8},{8,12},{12,16},{16,20},{20,24},{24,28},{1,5},{5,9},{9,... | collective-permute-start | bytes 4718600 | tf_op jit(solution)/shard_map/ppermute | solution.py:16
  11.0 1.3 collective-permute-start.1
  12.3 5.0 %collective-permute-start.2 = (f32[2,128]{1,0:T(2,128)S(1)}, f32[2,128]{1,0:T(2,128)S(1)}, u32[]{:S(2)}, u32[]{:S(2)}) collective-permute-start(f32[2,128]{1,0:T(2,128)S(1)} %get-tuple-element.9), channel_id=1, source_target_pairs={{0,4},{4,8},{8,12},{12,16},{16,20},{20,24},{24,28},{1,5},{5,9},{9,... | collective-permute-start | bytes 3080 | tf_op jit(solution)/shard_map/ppermute | solution.py:16
  17.4 1.3 collective-permute-start.3
  18.7 0.4 convert_element_type.26
  19.1 2.6 %collective-permute-done.3 = f32[2,128]{1,0:T(2,128)S(1)} collective-permute-done((f32[2,128]{1,0:T(2,128)S(1)}, f32[2,128]{1,0:T(2,128)S(1)}, u32[]{:S(2)}, u32[]{:S(2)}) %collective-permute-start.3) | collective-permute-done | bytes 1056 | tf_op jit(solution)/shard_map/ppermute | solution.py:19
  21.7 0.7 pad_maximum_fusion
  22.4 0.5 slice.98
  22.9 2.6 %fusion.4 = f32[32,32,9,128]{3,1,2,0:T(8,128)S(1)} fusion(f32[32,32,9,128]{3,1,2,0:T(8,128)S(1)} %slice.98, f32[32,32,11,128]{3,1,2,0:T(8,128)S(1)} %pad_maximum_fusion, f32[9,128]{1,0:T(8,128)S(1)} %pad_maximum_fusion.2), kind=kLoop, calls=%fused_computation.11 | loop fusion | flops 8257536 | bytes 18878976 | tf_op jit(solution)/shard_map/add | solution.py:40
  25.6 0.4 slice.101
  26.0 2.1 %fusion.9 = f32[32,32,7,128]{3,1,2,0:T(8,128)S(1)} fusion(f32[32,32,7,128]{3,1,2,0:T(8,128)S(1)} %slice.101, f32[32,32,9,128]{3,1,2,0:T(8,128)S(1)} %fusion.4, f32[7,128]{1,0:T(8,128)S(1)} %slice.102), kind=kLoop, calls=%fused_computation.17 | loop fusion | flops 6422528 | bytes 14683648 | tf_op jit(solution)/shard_map/add | solution.py:40
  28.0 0.2 slice.105
  28.3 1.4 fusion.16
  29.7 4.2 %copy.8 = f32[32,32,5,128]{3,2,1,0:T(8,128)} copy(f32[32,32,5,128]{3,1,2,0:T(8,128)S(1)} %fusion.16) | data formatting | bytes 5242880 | tf_op jit(solution)/shard_map/add | solution.py:40
  33.9 4.7 %reshape.136 = f32[32,32,640,1]{2,1,0,3:T(8,128)} reshape(f32[32,32,5,128]{3,2,1,0:T(8,128)} %copy.8) | data formatting | bytes 5242880 | tf_op jit(solution)/shard_map/reshape | solution.py:52
  38.6 3.2 %fusion.23 = f32[4,2,32,640]{3,0,2,1:T(4,128)S(1)} fusion(f32[32,32,640,1]{2,1,0,3:T(8,128)} %reshape.136, f32[4,1,32]{2,0,1:T(4,128)S(1)} %get-tuple-element.11, f32[4,1,32]{2,0,1:T(4,128)S(1)} %get-tuple-element.12), kind=kOutput, calls=%fused_computation.36 | convolution fusion | flops 62915072 | bytes 3277824 | tf_op jit(solution)/shard_map/ft,vtc->fvc/dot_general | solution.py:55
  41.9 16.4 %all_to_all.15 = f32[4,2,32,640]{3,2,1,0:T(8,128)S(1)} all-to-all(f32[4,2,32,640]{3,2,1,0:T(8,128)S(1)} %copy.9), channel_id=1, replica_groups=mesh['seabed'=8,'freq'=4] {'freq'}, dimensions={0} | all-to-all | bytes 1310720 | tf_op jit(solution)/shard_map/all_to_all | solution.py:57
  58.3 3.1 %fusion.17 = f32[128,1,2,2,600]{0,4,3,2,1:T(8,128)S(1)} fusion(f32[2,128,640,1]{2,1,3,0:T(8,128)S(1)} %bitcast.33, f32[1,2,600,640]{3,2,1,0:T(8,128)S(1)} %copy-done), kind=kOutput, calls=%fused_computation.27 | convolution fusion | flops 2359296000 | bytes 4956160 | tf_op jit(solution)/shard_map/kbvc,kasc->vkbas/dot_general | solution.py:58
  61.5 0.9 pad_maximum_fusion.1
  62.4 2.1 %copy.11 = f32[128,1,2,600]{3,2,1,0:T(2,128)} copy(f32[128,1,2,600]{0,3,2,1:T(8,128)} %pad_maximum_fusion.1) | data formatting | bytes 1228800 | tf_op jit(solution)/shard_map/stack | solution.py:62
  64.5 0.6 dynamic-slice
  65.8 84.9 %all-reduce.6.cloned.1.call-done = f32[128,1,2,600]{3,2,1,0:T(2,128)} async-done(((f32[128,1,2,600]{3,2,1,0:T(2,128)}), f32[128,1,2,600]{3,2,1,0:T(2,128)}) %all-reduce.6.cloned.1.call-update) | async-done | bytes 614416
  150.7 1.5 constant_dynamic-slice_fusion
  (20 shorter events, 0.3 us)
Async XLA Ops:
  6.5 51.8 %copy-start = (f32[1,2,600,640]{3,2,1,0:T(8,128)S(1)}, f32[1,2,600,640]{3,2,1,0:T(8,128)}, u32[]{:S(2)}) copy-start(f32[1,2,600,640]{3,2,1,0:T(8,128)} %param.5) | copy-start | bytes 9216004
  6.5 5.8 %copy-start.2 = (f32[5,128]{1,0:T(8,128)S(1)}, f32[5,128]{1,0:T(8,128)}, u32[]{:S(2)}) copy-start(f32[5,128]{1,0:T(8,128)} %param.4) | copy-start | bytes 7684
  6.5 144.1 %all-reduce.6.cloned.1.call-start = ((), (), s32[]{:S(2)}) async-start(), calls=%async_computation.1 | async-start | bytes 1310720
  6.5 12.2 %copy-start.1 = (bf16[32,32,5,128]{3,1,2,0:T(8,128)(2,1)S(1)}, bf16[32,32,5,128]{3,1,2,0:T(8,128)(2,1)}, u32[]{:S(2)}) copy-start(bf16[32,32,5,128]{3,1,2,0:T(8,128)(2,1)} %param.3) | copy-start | bytes 3932164
  8.5 13.2 %collective-permute-start = (f32[32,32,3,128]{3,1,2,0:T(8,128)S(1)}, f32[32,32,3,128]{3,1,2,0:T(8,128)S(1)}, u32[]{:S(2)}, u32[]{:S(2)}) collective-permute-start(f32[32,32,3,128]{3,1,2,0:T(8,128)S(1)} %get-tuple-element.5), channel_id=1, source_target_pairs={{0,4},{4,8},{8,12},{12,16},{16,20},{20,24},{24,28},{1,5},{5,9},{9,... | collective-permute-start | bytes 4718600 | tf_op jit(solution)/shard_map/ppermute | solution.py:16
  11.0 10.7 %collective-permute-start.1 = (f32[32,32,3,128]{3,1,2,0:T(8,128)S(1)}, f32[32,32,3,128]{3,1,2,0:T(8,128)S(1)}, u32[]{:S(2)}, u32[]{:S(2)}) collective-permute-start(f32[32,32,3,128]{3,1,2,0:T(8,128)S(1)} %get-tuple-element.6), channel_id=1, source_target_pairs={{4,0},{8,4},{12,8},{16,12},{20,16},{24,20},{28,24},{5,1},{9,5},{13... | collective-permute-start | bytes 4718600 | tf_op jit(solution)/shard_map/ppermute | solution.py:19
  12.3 6.8 %collective-permute-start.2 = (f32[2,128]{1,0:T(2,128)S(1)}, f32[2,128]{1,0:T(2,128)S(1)}, u32[]{:S(2)}, u32[]{:S(2)}) collective-permute-start(f32[2,128]{1,0:T(2,128)S(1)} %get-tuple-element.9), channel_id=1, source_target_pairs={{0,4},{4,8},{8,12},{12,16},{16,20},{20,24},{24,28},{1,5},{5,9},{9,... | collective-permute-start | bytes 3080 | tf_op jit(solution)/shard_map/ppermute | solution.py:16
  17.4 4.3 %collective-permute-start.3 = (f32[2,128]{1,0:T(2,128)S(1)}, f32[2,128]{1,0:T(2,128)S(1)}, u32[]{:S(2)}, u32[]{:S(2)}) collective-permute-start(f32[2,128]{1,0:T(2,128)S(1)} %get-tuple-element.10), channel_id=1, source_target_pairs={{4,0},{8,4},{12,8},{16,12},{20,16},{24,20},{28,24},{5,1},{9,5},{13... | collective-permute-start | bytes 3080 | tf_op jit(solution)/shard_map/ppermute | solution.py:19
  61.5 3.1 %copy-start.3 = (u32[32]{0:T(128)S(1)}, u32[32]{0:T(128)}, u32[]{:S(2)}) copy-start(u32[32]{0:T(128)} %constant.37) | copy-start | bytes 388
Sparse Core Ops, SparseCore 0:
  64.6 85.9 all-reduce.5
where the time goes:
time: 159 us
  waiting for transfers between devices  87.5 us (55%)
  blocking collectives  16.4 us (10%)
  local copies, waits for them, and re-layouts  16.3 us (10%)
  between operations  14.3 us (9%)
  starting transfers between devices  10.1 us (6%)
  other arithmetic  8.15 us (5%)
  matrix products  6.35 us (4%)
    unnamed x2, waiting for transfers between devices  84.9 us
    all_to_all x1, blocking collectives, shards(): lax.all_to_all(spectrum, 'freq', split_axis=0, concat_axis=2, tiled=True)  16.4 us
    ppermute x2, starting transfers between devices, with_halo(): lax.ppermute(lax.slice_in_dim(block, block.shape[dim] - width, None, axis...  7.52 us
    add x3, other arithmetic, relax(): return centre + rows_coefficient * (beside - 4.0 * centre)  6.11 us
    reshape x1, local copies, waits for them, and re-layouts, shards(): flat = field.reshape(vectors, steps_count, rows * width)  4.7 us
    add x1, local copies, waits for them, and re-layouts, relax(): return centre + rows_coefficient * (beside - 4.0 * centre)  4.19 us
    dot_general x1, matrix products, shards(): jnp.einsum('ft,vtc->fvc', table, flat, precision=lax.Precision.HIGHEST)  3.21 us
  transfers between devices with their start and end apart: 5, of which 2 were waited for; matrix products, arithmetic and copies ran while one was open for 1% of the time, Pallas kernels for 0%

commit v1 on v0

--- a/solution.py
+++ b/solution.py
@@ -54,7 +54,10 @@
     table = dft_table(steps_count, freq_count)
     spectrum = jnp.einsum("ft,vtc->fvc", table, flat, precision=lax.Precision.HIGHEST)
     spectrum = spectrum.reshape(freq_count, 2, vectors, rows * width)
-    regrouped = lax.all_to_all(spectrum, "freq", split_axis=0, concat_axis=2, tiled=True)
+    regrouped = jnp.concatenate(
+        lax.all_to_all(jnp.stack(jnp.split(spectrum, lax.axis_size("freq"), axis=0)), "freq", 0, 0),
+        axis=2,
+    )
     products = jnp.einsum("kbvc,kasc->vkbas", regrouped, transfer, precision=lax.Precision.HIGHEST)
     real_part = products[:, :, 0, 0] - products[:, :, 1, 1]
     imag_part = products[:, :, 1, 0] + products[:, :, 0, 1]

time: 159 us -> 149 us (0.937)
  local copies, waits for them, and re-layouts: 16.3 us -> 7.54 us
    reshape x1 -> x0, local copies, waits for them, and re-layouts: 4.7 us -> none  [shards(): flat = field.reshape(vectors, steps_count, rows * width)]
    add x1 -> x0, local copies, waits for them, and re-layouts: 4.19 us -> none  [relax(): return centre + rows_coefficient * (beside - 4.0 * centre)]
    add x3 -> x2, other arithmetic: 6.11 us -> 4.71 us  [relax(): return centre + rows_coefficient * (beside - 4.0 * centre)]
where the time goes in v1:
time: 149 us; the launch traced here: 148 us
  waiting for transfers between devices  87.5 us (59%)
  blocking collectives  16.4 us (11%)
  between operations  14.3 us (10%)
  starting transfers between devices  10.1 us (7%)
  local copies, waits for them, and re-layouts  7.54 us (5%)
  other arithmetic  7.01 us (5%)
  matrix products  5.66 us (4%)
    unnamed x2, waiting for transfers between devices  84.9 us
    all_to_all x1, blocking collectives, shards(): lax.all_to_all(jnp.stack(jnp.split(spectrum, lax.axis_size('freq'), axis=...  16.4 us
    ppermute x2, starting transfers between devices, with_halo(): lax.ppermute(lax.slice_in_dim(block, block.shape[dim] - width, None, axis...  7.52 us
    add x2, other arithmetic, relax(): return centre + rows_coefficient * (beside - 4.0 * centre)  4.71 us
    dot_general x1, matrix products, shards(): jnp.einsum('kbvc,kasc->vkbas', regrouped, transfer, precision=lax.Precisi...  3.14 us
  transfers between devices with their start and end apart: 5, of which 2 were waited for; matrix products, arithmetic and copies ran while one was open for 1% of the time, Pallas kernels for 0%

profile of v1, /device:TPU:0, one launch (start us, length us, event | category | flops | bytes accessed | tf_op | source)
XLA Modules:
  0.0 148.4 jit_solution(7739391057713477806)
XLA Ops:
  6.5 2.0 %fusion.31 = (f32[32,32,3,128]{3,1,2,0:T(8,128)S(1)}, f32[32,32,3,128]{3,1,2,0:T(8,128)S(1)}) fusion(bf16[32,32,5,128]{3,1,2,0:T(8,128)(2,1)} %param.3), kind=kLoop, calls=%fused_computation.54 | loop fusion | bytes 6291456 | tf_op jit(solution)/shard_map/slice | solution.py:17
  8.5 2.5 %collective-permute-start = (f32[32,32,3,128]{3,1,2,0:T(8,128)S(1)}, f32[32,32,3,128]{3,1,2,0:T(8,128)S(1)}, u32[]{:S(2)}, u32[]{:S(2)}) collective-permute-start(f32[32,32,3,128]{3,1,2,0:T(8,128)S(1)} %get-tuple-element.5), channel_id=1, source_target_pairs={{0,4},{4,8},{8,12},{12,16},{16,20},{20,24},{24,28},{1,5},{5,9},{9,... | collective-permute-start | bytes 4718600 | tf_op jit(solution)/shard_map/ppermute | solution.py:16
  11.0 1.3 collective-permute-start.1
  12.3 5.0 %collective-permute-start.2 = (f32[2,128]{1,0:T(2,128)S(1)}, f32[2,128]{1,0:T(2,128)S(1)}, u32[]{:S(2)}, u32[]{:S(2)}) collective-permute-start(f32[2,128]{1,0:T(2,128)S(1)} %get-tuple-element.13), channel_id=1, source_target_pairs={{0,4},{4,8},{8,12},{12,16},{16,20},{20,24},{24,28},{1,5},{5,9},{9,... | collective-permute-start | bytes 3080 | tf_op jit(solution)/shard_map/ppermute | solution.py:16
  17.4 1.3 collective-permute-start.3
  18.7 0.4 convert_element_type.26
  19.1 2.5 %collective-permute-done.3 = f32[2,128]{1,0:T(2,128)S(1)} collective-permute-done((f32[2,128]{1,0:T(2,128)S(1)}, f32[2,128]{1,0:T(2,128)S(1)}, u32[]{:S(2)}, u32[]{:S(2)}) %collective-permute-start.3) | collective-permute-done | bytes 1056 | tf_op jit(solution)/shard_map/ppermute | solution.py:19
  21.7 0.6 pad_maximum_fusion
  22.4 0.5 slice.102
  22.9 2.6 %fusion.4 = f32[32,32,9,128]{3,1,2,0:T(8,128)S(1)} fusion(f32[32,32,9,128]{3,1,2,0:T(8,128)S(1)} %slice.102, f32[32,32,11,128]{3,1,2,0:T(8,128)S(1)} %pad_maximum_fusion, f32[9,128]{1,0:T(8,128)S(1)} %pad_maximum_fusion.3), kind=kLoop, calls=%fused_computation.11 | loop fusion | flops 8257536 | bytes 18878976 | tf_op jit(solution)/shard_map/add | solution.py:40
  25.5 0.4 slice.105
  25.9 2.1 %fusion.9 = f32[32,32,7,128]{3,1,2,0:T(8,128)S(1)} fusion(f32[32,32,7,128]{3,1,2,0:T(8,128)S(1)} %slice.105, f32[32,32,9,128]{3,1,2,0:T(8,128)S(1)} %fusion.4, f32[7,128]{1,0:T(8,128)S(1)} %slice.106), kind=kLoop, calls=%fused_computation.17 | loop fusion | flops 6422528 | bytes 14683648 | tf_op jit(solution)/shard_map/add | solution.py:40
  28.0 0.2 slice.109
  28.3 2.5 %fusion.18 = f32[8,32,640]{2,0,1:T(8,128)S(1)} fusion(f32[8,32,1]{1,0,2:T(8,128)S(1)} %bitcast.42, f32[32,32,5,128]{3,1,2,0:T(8,128)S(1)} %slice.109, f32[32,32,7,128]{3,1,2,0:T(8,128)S(1)} %fusion.9, f32[5,128]{1,0:T(8,128)S(1)} %copy-done.2), kind=kOutput, calls=%fused_computation.27 | convolution fusion | flops 67502080 | bytes 8527872 | tf_op jit(solution)/shard_map/ft,vtc->fvc/dot_general | solution.py:55
  30.8 0.2 slice_bitcast_fusion.3
  31.0 0.3 pad_maximum_fusion.1
  31.3 16.4 %all_to_all.5 = f32[4,1,2,32,640]{4,2,3,1,0:T(2,128)S(1)} all-to-all(f32[4,1,2,32,640]{4,2,3,1,0:T(2,128)S(1)} %pad_maximum_fusion.1), channel_id=1, replica_groups=mesh['seabed'=8,'freq'=4] {'freq'}, dimensions={0} | all-to-all | bytes 1310720 | tf_op jit(solution)/shard_map/all_to_all | solution.py:58
  47.7 3.1 %fusion.21 = f32[128,1,2,2,600]{0,4,3,2,1:T(8,128)S(1)} fusion(f32[1,2,600,640]{3,2,1,0:T(8,128)S(1)} %copy-done, f32[2,128,640,1]{2,0,1,3:T(2,128)S(1)} %bitcast.41), kind=kOutput, calls=%fused_computation.31 | convolution fusion | flops 2359296000 | bytes 4956160 | tf_op jit(solution)/shard_map/kbvc,kasc->vkbas/dot_general | solution.py:61
  50.9 0.1 fusion.26
  50.9 0.9 pad_maximum_fusion.2
  51.8 2.1 %copy.18 = f32[128,1,2,600]{3,2,1,0:T(2,128)} copy(f32[128,1,2,600]{0,3,2,1:T(8,128)} %pad_maximum_fusion.2) | data formatting | bytes 1228800 | tf_op jit(solution)/shard_map/stack | solution.py:65
  53.9 0.6 dynamic-slice
  55.1 84.9 %all-reduce.6.cloned.1.call-done = f32[128,1,2,600]{3,2,1,0:T(2,128)} async-done(((f32[128,1,2,600]{3,2,1,0:T(2,128)}), f32[128,1,2,600]{3,2,1,0:T(2,128)}) %all-reduce.6.cloned.1.call-update) | async-done | bytes 614416
  140.0 1.5 %constant_dynamic-slice_fusion = f32[16,1,2,600]{3,2,1,0:T(2,128)} fusion(f32[128,1,2,600]{3,2,1,0:T(2,128)} %all-reduce.6.cloned.1.call-done, u32[]{:T(128)S(6)} %multiply.1), kind=kLoop, calls=%fused_computation.53 | loop fusion | bytes 153604
  (19 shorter events, 0.1 us)
Async XLA Ops:
  6.5 41.2 %copy-start = (f32[1,2,600,640]{3,2,1,0:T(8,128)S(1)}, f32[1,2,600,640]{3,2,1,0:T(8,128)}, u32[]{:S(2)}) copy-start(f32[1,2,600,640]{3,2,1,0:T(8,128)} %param.5) | copy-start | bytes 9216004
  6.5 5.8 %copy-start.2 = (f32[5,128]{1,0:T(8,128)S(1)}, f32[5,128]{1,0:T(8,128)}, u32[]{:S(2)}) copy-start(f32[5,128]{1,0:T(8,128)} %param.4) | copy-start | bytes 7684
  6.5 133.5 %all-reduce.6.cloned.1.call-start = ((), (), s32[]{:S(2)}) async-start(), calls=%async_computation.1 | async-start | bytes 1310720
  6.5 12.2 %copy-start.1 = (bf16[32,32,5,128]{3,1,2,0:T(8,128)(2,1)S(1)}, bf16[32,32,5,128]{3,1,2,0:T(8,128)(2,1)}, u32[]{:S(2)}) copy-start(bf16[32,32,5,128]{3,1,2,0:T(8,128)(2,1)} %param.3) | copy-start | bytes 3932164
  8.5 13.2 %collective-permute-start = (f32[32,32,3,128]{3,1,2,0:T(8,128)S(1)}, f32[32,32,3,128]{3,1,2,0:T(8,128)S(1)}, u32[]{:S(2)}, u32[]{:S(2)}) collective-permute-start(f32[32,32,3,128]{3,1,2,0:T(8,128)S(1)} %get-tuple-element.5), channel_id=1, source_target_pairs={{0,4},{4,8},{8,12},{12,16},{16,20},{20,24},{24,28},{1,5},{5,9},{9,... | collective-permute-start | bytes 4718600 | tf_op jit(solution)/shard_map/ppermute | solution.py:16
  11.0 10.7 %collective-permute-start.1 = (f32[32,32,3,128]{3,1,2,0:T(8,128)S(1)}, f32[32,32,3,128]{3,1,2,0:T(8,128)S(1)}, u32[]{:S(2)}, u32[]{:S(2)}) collective-permute-start(f32[32,32,3,128]{3,1,2,0:T(8,128)S(1)} %get-tuple-element.6), channel_id=1, source_target_pairs={{4,0},{8,4},{12,8},{16,12},{20,16},{24,20},{28,24},{5,1},{9,5},{13... | collective-permute-start | bytes 4718600 | tf_op jit(solution)/shard_map/ppermute | solution.py:19
  12.3 6.8 %collective-permute-start.2 = (f32[2,128]{1,0:T(2,128)S(1)}, f32[2,128]{1,0:T(2,128)S(1)}, u32[]{:S(2)}, u32[]{:S(2)}) collective-permute-start(f32[2,128]{1,0:T(2,128)S(1)} %get-tuple-element.13), channel_id=1, source_target_pairs={{0,4},{4,8},{8,12},{12,16},{16,20},{20,24},{24,28},{1,5},{5,9},{9,... | collective-permute-start | bytes 3080 | tf_op jit(solution)/shard_map/ppermute | solution.py:16
  17.4 4.3 %collective-permute-start.3 = (f32[2,128]{1,0:T(2,128)S(1)}, f32[2,128]{1,0:T(2,128)S(1)}, u32[]{:S(2)}, u32[]{:S(2)}) collective-permute-start(f32[2,128]{1,0:T(2,128)S(1)} %get-tuple-element.14), channel_id=1, source_target_pairs={{4,0},{8,4},{12,8},{16,12},{20,16},{24,20},{28,24},{5,1},{9,5},{13... | collective-permute-start | bytes 3080 | tf_op jit(solution)/shard_map/ppermute | solution.py:19
  50.8 3.1 %copy-start.3 = (u32[32]{0:T(128)S(1)}, u32[32]{0:T(128)}, u32[]{:S(2)}) copy-start(u32[32]{0:T(128)} %constant.37) | copy-start | bytes 388
Sparse Core Ops, SparseCore 0:
  54.0 85.9 all-reduce.5
